TPU v7x, 256 devices: a whole 4x4x8 slice. The times are simulated.
256 devices in a mesh: sec: 32 (over z, y), blk: 8 (over x, core).
Axes of the slice: x: 4, y: 4, z: 8, core: 2. Of those that a mesh axis runs over, the one named last changes fastest.
Arguments:
- state_now: float32 [128, 65536], P(None, ('sec', 'blk')), may hold values from -5 to 5
- source: float32 [128, 65536], P(None, ('sec', 'blk')), may hold values from -6 to 6
- fan_gain: float32 [65536], P(('sec', 'blk')), may hold values from 0.5 to 12
- section_block: bfloat16 [65536, 2048], P(('sec', 'blk')), may hold values from -1 to 7
- block_inverse: bfloat16 [65536, 2048], P(('sec', 'blk')), may hold values from -1 to 1
- back_panel: bfloat16 [65536, 128], P(('sec', 'blk')), may hold values from -6 to 6
- ahead_panel: bfloat16 [65536, 128], P(('sec', 'blk')), may hold values from -0.0625 to 0.0625
- interface: int32 [32, 128], P('sec'), may hold values from 0 to 2047, as said below
Outputs:
- new_state: float32 [128, 65536], P(None, ('sec', 'blk'))
Inputs may be any that keep to these rules, and one draw needn't show every extreme that they name: `interface`: entries of one section are distinct; entry p lies in [p * 16, (p + 1) * 16).
All inputs are finite; a program needn't handle non-finite values.
Results may differ from a plain program's by a relative error of at most 0.0063.
Values may be sent and summed in bfloat16 or wider, within the bound.
A program may use at most 64 MiB of HBM per device.

v0:
```python
import jax
import jax.numpy as jnp
from jax import lax
from jax.sharding import PartitionSpec as P

KRYLOV = 3
epsilon = 1e-06


def extended(x, sides, width):
    for axis, dim in sides:
        size, length = (lax.axis_size(axis), x.shape[dim])
        up = [(i, (i + 1) % size) for i in range(size - 1)]
        down = [(j, i) for i, j in up]
        last = lax.slice_in_dim(x, length - width, length, axis=dim)
        first = lax.slice_in_dim(x, 0, width, axis=dim)
        before = lax.ppermute(last, axis, up)
        after = lax.ppermute(first, axis, down)
        x = jnp.concatenate([before, x, after], axis=dim)
    return x


def entering(value, axis, join, neutral):
    count, mine = (lax.axis_size(axis), lax.axis_index(axis))
    pieces = jax.tree.map(lambda part: lax.all_gather(part, axis), value)
    so_far = jax.tree.map(
        lambda part, zero: jnp.full_like(part, 0) + jnp.asarray(zero, part.dtype), value, neutral
    )

    def step(position, so_far):
        longer = join(so_far, jax.tree.map(lambda part: part[position], pieces))
        return jax.tree.map(lambda new, old: jnp.where(position < mine, new, old), longer, so_far)

    return lax.fori_loop(0, count - 1, step, so_far)


def least_squares(hessen, beta):
    cases = hessen.shape[0]
    depth = hessen.shape[2]
    rhs = jnp.zeros((cases, depth + 1), jnp.float32).at[:, 0].set(beta)
    upper = hessen
    for column in range(depth):
        upper_row = upper[:, column, :]
        lower_row = upper[:, column + 1, :]
        radius = jnp.sqrt(upper_row[:, column] ** 2 + lower_row[:, column] ** 2)
        cosine = upper_row[:, column] / radius
        sine_term = lower_row[:, column] / radius
        upper = upper.at[:, column, :].set(
            cosine[:, None] * upper_row + sine_term[:, None] * lower_row
        )
        upper = upper.at[:, column + 1, :].set(
            -sine_term[:, None] * upper_row + cosine[:, None] * lower_row
        )
        first_rhs = rhs[:, column]
        second_rhs = rhs[:, column + 1]
        rhs = rhs.at[:, column].set(cosine * first_rhs + sine_term * second_rhs)
        rhs = rhs.at[:, column + 1].set(-sine_term * first_rhs + cosine * second_rhs)
    weights = jnp.zeros((cases, depth), jnp.float32)
    for column in reversed(range(depth)):
        remain = rhs[:, column] - jnp.sum(
            upper[:, column, column + 1 :] * weights[:, column + 1 :], axis=1
        )
        weights = weights.at[:, column].set(remain / upper[:, column, column])
    return weights


def local(
    state_now, source, fan_gain, section_block, block_inverse, back_panel, ahead_panel, interface
):
    highest = lax.Precision.HIGHEST
    cases, node_rows = state_now.shape
    panel_width = back_panel.shape[1]
    indices = interface[0]
    first_row = lax.axis_index("blk") * node_rows
    selector = (indices[None, :] == first_row + jnp.arange(node_rows)[:, None]).astype(jnp.float32)
    contract = (((1,), (1,)), ((), ()))
    gain_panel = jnp.dot(
        block_inverse,
        lax.all_gather(back_panel, "blk", axis=0, tiled=True),
        preferred_element_type=jnp.float32,
    )
    panel_maps = -lax.psum(jnp.dot(selector.T, gain_panel, precision=highest), "blk")

    def section_terms(dense_part, behind_vals, piece):
        width = piece.shape[1]
        dense_part = lax.dot_general(
            piece, section_block, contract, preferred_element_type=jnp.float32
        )
        picker = (indices[None, :] == jnp.arange(width)[:, None]).astype(jnp.bfloat16)
        behind_vals = jnp.dot(piece, picker, preferred_element_type=jnp.float32)
        return (dense_part, behind_vals)

    def fold_section(carry, piece):
        return section_terms(carry[0], carry[1], piece)

    def operator(vector):
        rounded = vector.astype(jnp.bfloat16)
        empty_dense = jnp.zeros((cases, node_rows), jnp.float32)
        empty_panel = jnp.zeros((cases, panel_width), jnp.float32)
        start_carry = (empty_dense, empty_panel)
        folded = fold_section(start_carry, lax.all_gather(rounded, "blk", axis=1, tiled=True))
        dense_part, behind_vals = folded
        upward = lax.psum(jnp.dot(rounded, ahead_panel, preferred_element_type=jnp.float32), "blk")
        framed = extended(jnp.stack([behind_vals, upward])[None], (("sec", 0),), 1)
        behind = framed[0, 0].astype(jnp.bfloat16)
        ahead_term = framed[2, 1]
        lower_term = lax.dot_general(
            behind, back_panel, contract, preferred_element_type=jnp.float32
        )
        upper_term = jnp.dot(ahead_term, selector.T, precision=highest)
        return dense_part + lower_term + upper_term

    def compose(earlier, later):
        first_map, first_value = earlier
        second_map, second_value = later
        joined_map = jnp.dot(second_map, first_map, precision=highest)
        joined_value = jnp.dot(first_value, second_map.T, precision=highest) + second_value
        return (joined_map, joined_value)

    def lengths(vector):
        return jnp.sqrt(lax.psum(jnp.sum(vector * vector, axis=1), ("sec", "blk")) + epsilon)

    bent = jnp.tanh(state_now)
    residual = source - operator(state_now) - fan_gain[None, :] * bent
    jac_diag = fan_gain[None, :] * (1.0 - bent * bent)
    beta = lengths(residual)
    basis = [residual / beta[:, None]]
    directions = []
    hessen = jnp.zeros((cases, KRYLOV + 1, KRYLOV), jnp.float32)
    for column in range(KRYLOV):
        precondition_rounded = basis[column].astype(jnp.bfloat16)
        precondition_folded = lax.dot_general(
            lax.all_gather(precondition_rounded, "blk", axis=1, tiled=True),
            block_inverse,
            contract,
            preferred_element_type=jnp.float32,
        )
        values = lax.psum(jnp.dot(precondition_folded, selector, precision=highest), "blk")
        identity = (
            jnp.eye(panel_width, dtype=jnp.float32),
            jnp.zeros((cases, panel_width), jnp.float32),
        )
        _, before = entering((panel_maps, values), "sec", compose, identity)
        direction = precondition_folded - lax.dot_general(
            before, gain_panel, contract, precision=highest
        )
        product = operator(direction) + jac_diag * direction
        stacked = jnp.stack(basis)
        projections = lax.psum(jnp.sum(product[None] * stacked, axis=2), ("sec", "blk"))
        product = product - jnp.sum(projections[:, :, None] * stacked, axis=0)
        length = lengths(product)
        hessen = hessen.at[:, : column + 1, column].set(projections.T)
        hessen = hessen.at[:, column + 1, column].set(length)
        basis.append(product / length[:, None])
        directions.append(direction)
    weights = least_squares(hessen, beta)
    update = jnp.zeros_like(state_now)
    for column in range(KRYLOV):
        update = update + weights[:, column : column + 1] * directions[column]
    return state_now + update


def solution(mesh):
    in_specs = (
        P(None, ("sec", "blk")),
        P(None, ("sec", "blk")),
        P(("sec", "blk")),
        P(("sec", "blk"), None),
        P(("sec", "blk"), None),
        P(("sec", "blk"), None),
        P(("sec", "blk"), None),
        P("sec", None),
    )
    out_specs = P(None, ("sec", "blk"))
    return jax.shard_map(local, mesh=mesh, in_specs=in_specs, out_specs=out_specs, check_vma=False)
```

profile of v0, /device:TPU:1, one launch (start us, length us, event | category | flops | bytes accessed | tf_op | source)
XLA Modules:
  0.0 1640.1 jit_solution(12427240941463223437)
XLA Ops:
  9.4 16.2 all_gather.52
  27.1 13.1 all_gather.54
  40.7 34.6 %all-reduce.11.cloned.1.call-done = f32[1,128,128]{1,2,0:T(8,128)} async-done(((f32[1,128,128]{1,2,0:T(8,128)}), f32[1,128,128]{1,2,0:T(8,128)}) %all-reduce.11.cloned.1.call-update) | async-done | bytes 65552 | tf_op jit(solution)/shard_map/psum | solution.py:103
  86.3 83.2 %psum.106 = f32[128]{0:T(128)S(1)} all-reduce(f32[128]{0:T(128)S(1)} %get-tuple-element.720), channel_id=1, replica_groups=mesh['sec'=32,'blk'=8] {'sec','blk'}, use_global_device_ids=true, to_apply=%region_4.0 | all-reduce | flops 128 | bytes 1024 | tf_op jit(solution)/shard_map/psum | solution.py:121
  169.7 13.9 all_gather.53
  185.0 57.8 %all-reduce.23.cloned.1.call-done = (f32[128,128]{1,0:T(8,128)}, f32[1,128,128]{2,1,0:T(8,128)}) async-done(((f32[128,128]{1,0:T(8,128)}, f32[1,128,128]{2,1,0:T(8,128)}), (f32[128,128]{1,0:T(8,128)}, f32[1,128,128]{2,1,0:T(8,128)})) %all-reduce.23.cloned.1.call-update) | async-done | bytes 131088 | tf_op jit(solution)/shard_map/psum | solution.py:82
  244.9 75.7 %all-gather.12.cloned.1.call-done = f32[4096,128]{1,0:T(8,128)} async-done(((f32[128,128]{1,0:T(8,128)}), f32[4096,128]{1,0:T(8,128)}) %all-gather.12.cloned.1.call-update) | async-done | bytes 2097168 | tf_op jit(solution)/shard_map/all_gather | solution.py:25
  320.6 77.6 %all-gather.6.cloned.1.call-done = f32[32,128,128]{2,1,0:T(8,128)} async-done(((f32[1,128,128]{2,1,0:T(8,128)}), f32[32,128,128]{2,1,0:T(8,128)}) %all-gather.6.cloned.1.call-update) | async-done | bytes 2097168 | tf_op jit(solution)/shard_map/all_gather | solution.py:25
  398.3 63.2 %while.64 = (s32[]{:T(128)}, f32[128,128]{0,1:T(8,128)S(1)}, s32[]{:T(128)}, f32[32,128,128]{2,1,0:T(8,128)}, f32[32,128,128]{2,1,0:T(8,128)}, /*index=5*/s32[]{:T(128)}, s32[]{:T(128)}) while((s32[]{:T(128)}, f32[128,128]{0,1:T(8,128)S(1)}, s32[]{:T(128)}, f32[32,128,128]{2,1,0:T(8,128)}, f32[32,128,128]{2,1,0:T(8,128)}, ...), condition=%wide.region_8.9_spmd.clone, body=%wide.region_7.8_spmd.clone.sunk | while | flops 25231364 | bytes 723043 | solution.py:34
  461.8 17.8 %all_gather.59 = bf16[128,2048]{1,0:T(8,128)(2,1)S(1)} all-gather(bf16[128,256]{1,0:T(8,128)(2,1)S(1)} %get-tuple-element.722), channel_id=1, replica_groups=mesh['sec'=32,'blk'=8] {'blk'}, dimensions={1}, use_global_device_ids=true | all-gather | bytes 589824 | tf_op jit(solution)/shard_map/all_gather | solution.py:101
  480.8 57.6 %all-reduce.13.cloned.1.call-done = f32[1,128,128]{2,1,0:T(8,128)} async-done(((f32[1,128,128]{2,1,0:T(8,128)}), f32[1,128,128]{2,1,0:T(8,128)}) %all-reduce.13.cloned.1.call-update) | async-done | bytes 65552 | tf_op jit(solution)/shard_map/psum | solution.py:103
  544.4 4.2 collective-permute-done.3
  549.1 83.2 %psum.110 = f32[1,128]{1,0:T(1,128)S(1)} all-reduce(f32[1,128]{1,0:T(1,128)S(1)} %bitcast.287), channel_id=1, replica_groups=mesh['sec'=32,'blk'=8] {'sec','blk'}, use_global_device_ids=true, to_apply=%region_11.12 | all-reduce | flops 128 | bytes 1024 | tf_op jit(solution)/shard_map/psum | solution.py:149
  632.5 72.3 %psum.111 = f32[128]{0:T(128)S(1)} all-reduce(f32[128]{0:T(128)S(1)} %get-tuple-element.687), channel_id=1, replica_groups=mesh['sec'=32,'blk'=8] {'sec','blk'}, use_global_device_ids=true, to_apply=%region_13.14 | all-reduce | flops 128 | bytes 1024 | tf_op jit(solution)/shard_map/psum | solution.py:121
  705.0 13.6 all_gather.60
  720.1 58.5 %all-reduce.15.cloned.1.call-done = f32[1,128,128]{2,1,0:T(8,128)} async-done(((f32[1,128,128]{2,1,0:T(8,128)}), f32[1,128,128]{2,1,0:T(8,128)}) %all-reduce.15.cloned.1.call-update) | async-done | bytes 65552 | tf_op jit(solution)/shard_map/psum | solution.py:138
  778.7 77.7 %all-gather.8.cloned.1.call-done = f32[32,128,128]{2,1,0:T(8,128)} async-done(((f32[1,128,128]{2,1,0:T(8,128)}), f32[32,128,128]{2,1,0:T(8,128)}) %all-gather.8.cloned.1.call-update) | async-done | bytes 2097168 | tf_op jit(solution)/shard_map/all_gather | solution.py:25
  856.4 63.2 %while.65 = (s32[]{:T(128)}, f32[128,128]{0,1:T(8,128)S(1)}, s32[]{:T(128)}, f32[32,128,128]{2,1,0:T(8,128)}, f32[32,128,128]{2,1,0:T(8,128)}, /*index=5*/s32[]{:T(128)}, s32[]{:T(128)}) while((s32[]{:T(128)}, f32[128,128]{0,1:T(8,128)S(1)}, s32[]{:T(128)}, f32[32,128,128]{2,1,0:T(8,128)}, f32[32,128,128]{2,1,0:T(8,128)}, ...), condition=%wide.region_16.17_spmd.clone, body=%wide.region_15.16_spmd.clone.sunk | while | flops 25231364 | bytes 723043 | solution.py:34
  920.6 17.8 %all_gather.63 = bf16[128,2048]{1,0:T(8,128)(2,1)S(1)} all-gather(bf16[128,256]{1,0:T(8,128)(2,1)S(1)} %get-tuple-element.724), channel_id=1, replica_groups=mesh['sec'=32,'blk'=8] {'blk'}, dimensions={1}, use_global_device_ids=true | all-gather | bytes 589824 | tf_op jit(solution)/shard_map/all_gather | solution.py:101
  939.7 57.4 %all-reduce.17.cloned.1.call-done = f32[1,128,128]{2,1,0:T(8,128)} async-done(((f32[1,128,128]{2,1,0:T(8,128)}), f32[1,128,128]{2,1,0:T(8,128)}) %all-reduce.17.cloned.1.call-update) | async-done | bytes 65552 | tf_op jit(solution)/shard_map/psum | solution.py:103
  1003.1 4.2 collective-permute-done.5
  1007.8 83.2 %psum.114 = f32[2,128]{1,0:T(2,128)S(1)} all-reduce(f32[2,128]{1,0:T(2,128)S(1)} %multiply_reduce_fusion.3), channel_id=1, replica_groups=mesh['sec'=32,'blk'=8] {'sec','blk'}, use_global_device_ids=true, to_apply=%region_19.20 | all-reduce | flops 256 | bytes 2048 | tf_op jit(solution)/shard_map/psum | solution.py:149
  1091.2 72.3 %psum.115 = f32[128]{0:T(128)S(1)} all-reduce(f32[128]{0:T(128)S(1)} %get-tuple-element.683), channel_id=1, replica_groups=mesh['sec'=32,'blk'=8] {'sec','blk'}, use_global_device_ids=true, to_apply=%region_22.23 | all-reduce | flops 128 | bytes 1024 | tf_op jit(solution)/shard_map/psum | solution.py:121
  1163.7 13.6 all_gather.64
  1178.8 58.5 %all-reduce.19.cloned.1.call-done = f32[1,128,128]{2,1,0:T(8,128)} async-done(((f32[1,128,128]{2,1,0:T(8,128)}), f32[1,128,128]{2,1,0:T(8,128)}) %all-reduce.19.cloned.1.call-update) | async-done | bytes 65552 | tf_op jit(solution)/shard_map/psum | solution.py:138
  1243.8 71.1 %all-gather.10.cloned.1.call-done = f32[32,128,128]{2,1,0:T(8,128)} async-done(((f32[1,128,128]{2,1,0:T(8,128)}), f32[32,128,128]{2,1,0:T(8,128)}) %all-gather.10.cloned.1.call-update) | async-done | bytes 2097168 | tf_op jit(solution)/shard_map/all_gather | solution.py:25
  1314.9 63.2 %while.66 = (s32[]{:T(128)}, f32[128,128]{0,1:T(8,128)S(1)}, s32[]{:T(128)}, f32[32,128,128]{2,1,0:T(8,128)}, f32[32,128,128]{2,1,0:T(8,128)}, /*index=5*/s32[]{:T(128)}, s32[]{:T(128)}) while((s32[]{:T(128)}, f32[128,128]{0,1:T(8,128)S(1)}, s32[]{:T(128)}, f32[32,128,128]{2,1,0:T(8,128)}, f32[32,128,128]{2,1,0:T(8,128)}, ...), condition=%wide.region_26.27_spmd.clone, body=%wide.region_25.26_spmd.clone.sunk | while | flops 25231364 | bytes 723043 | solution.py:34
  1379.1 17.8 %all_gather.67 = bf16[128,2048]{1,0:T(8,128)(2,1)S(1)} all-gather(bf16[128,256]{1,0:T(8,128)(2,1)S(1)} %get-tuple-element.726), channel_id=1, replica_groups=mesh['sec'=32,'blk'=8] {'blk'}, dimensions={1}, use_global_device_ids=true | all-gather | bytes 589824 | tf_op jit(solution)/shard_map/all_gather | solution.py:101
  1398.0 57.6 %all-reduce.21.cloned.1.call-done = f32[1,128,128]{2,1,0:T(8,128)} async-done(((f32[1,128,128]{2,1,0:T(8,128)}), f32[1,128,128]{2,1,0:T(8,128)}) %all-reduce.21.cloned.1.call-update) | async-done | bytes 65552 | tf_op jit(solution)/shard_map/psum | solution.py:103
  1461.8 4.2 collective-permute-done.7
  1467.2 83.2 %psum.118 = f32[3,128]{1,0:T(4,128)S(1)} all-reduce(f32[3,128]{1,0:T(4,128)S(1)} %multiply_reduce_fusion.1), channel_id=1, replica_groups=mesh['sec'=32,'blk'=8] {'sec','blk'}, use_global_device_ids=true, to_apply=%region_29.30 | all-reduce | flops 384 | bytes 3072 | tf_op jit(solution)/shard_map/psum | solution.py:149
  1550.6 72.3 %psum.119 = f32[128]{0:T(128)S(1)} all-reduce(f32[128]{0:T(128)S(1)} %multiply_reduce_fusion.4), channel_id=1, replica_groups=mesh['sec'=32,'blk'=8] {'sec','blk'}, use_global_device_ids=true, to_apply=%region_32.33 | all-reduce | flops 128 | bytes 1024 | tf_op jit(solution)/shard_map/psum | solution.py:121
  (521 shorter events, 251.6 us)
Async XLA Ops:
  6.5 33.7 %copy-start = (bf16[256,2048]{1,0:T(8,128)(2,1)S(1)}, bf16[256,2048]{1,0:T(8,128)(2,1)}, u32[]{:S(2)}) copy-start(bf16[256,2048]{1,0:T(8,128)(2,1)} %param.62) | copy-start | bytes 3145732
  6.5 20.0 %copy-start.1 = (bf16[256,2048]{1,0:T(8,128)(2,1)S(1)}, bf16[256,2048]{1,0:T(8,128)(2,1)}, u32[]{:S(2)}) copy-start(bf16[256,2048]{1,0:T(8,128)(2,1)} %param.61) | copy-start | bytes 3145732
  6.5 20.6 %copy-start.3 = (bf16[256,128]{1,0:T(8,128)(2,1)S(1)}, bf16[256,128]{1,0:T(8,128)(2,1)}, u32[]{:S(2)}) copy-start(bf16[256,128]{1,0:T(8,128)(2,1)} %param.63) | copy-start | bytes 196612
  6.5 68.7 %all-reduce.11.cloned.1.call-start = ((), (), s32[]{:S(2)}) async-start(), calls=%async_computation | async-start | bytes 131072 | tf_op jit(solution)/shard_map/psum | solution.py:103
  9.3 233.5 %all-reduce.23.cloned.1.call-start = ((), (), s32[]{:S(2)}) async-start(), calls=%async_computation.10 | async-start | bytes 262144 | tf_op jit(solution)/shard_map/psum | solution.py:82
  26.6 52.7 %copy-start.9 = (s32[1,128]{1,0:T(1,128)S(1)}, s32[1,128]{1,0:T(1,128)}, u32[]{:S(2)}) copy-start(s32[1,128]{1,0:T(1,128)} %param.65) | copy-start | bytes 1540
  26.6 59.3 %copy-start.2 = (f32[128,256]{1,0:T(8,128)S(1)}, f32[128,256]{1,0:T(8,128)}, u32[]{:S(2)}) copy-start(f32[128,256]{1,0:T(8,128)} %param.58) | copy-start | bytes 393220
  26.6 59.3 %copy-start.8 = (f32[128,256]{1,0:T(8,128)S(1)}, f32[128,256]{1,0:T(8,128)}, u32[]{:S(2)}) copy-start(f32[128,256]{1,0:T(8,128)} %param.59) | copy-start | bytes 393220
  26.6 59.3 %copy-start.10 = (f32[256]{0:T(256)S(1)}, f32[256]{0:T(256)}, u32[]{:S(2)}) copy-start(f32[256]{0:T(256)} %param.60) | copy-start | bytes 3076
  76.1 5.4 collective-permute-start
  80.2 5.7 collective-permute-start.1
  169.6 228.7 %copy-start.11 = (f32[128]{0:T(128)}, f32[128]{0:T(128)S(1)}, u32[]{:S(2)}) copy-start(f32[128]{0:T(128)S(1)} %psum.106) | copy-start | bytes 1540
  185.0 135.7 %all-gather.12.cloned.1.call-start = ((), (), s32[]{:S(2)}) async-start(), calls=%async_computation.9 | async-start | bytes 2162688 | tf_op jit(solution)/shard_map/all_gather | solution.py:25
  244.3 154.0 %all-gather.6.cloned.1.call-start = ((), (), s32[]{:S(2)}) async-start(), calls=%async_computation.1 | async-start | bytes 2162688 | tf_op jit(solution)/shard_map/all_gather | solution.py:25
  244.9 293.6 %all-reduce.13.cloned.1.call-start = ((), (), s32[]{:S(2)}) async-start(), calls=%async_computation.2 | async-start | bytes 131072 | tf_op jit(solution)/shard_map/psum | solution.py:103
  398.3 81.4 %copy-start.7 = (bf16[256,128]{1,0:T(8,128)(2,1)S(1)}, bf16[256,128]{1,0:T(8,128)(2,1)}, u32[]{:S(2)}) copy-start(bf16[256,128]{1,0:T(8,128)(2,1)} %param.64) | copy-start | bytes 196612
  480.4 298.2 %all-reduce.15.cloned.1.call-start = ((), (), s32[]{:S(2)}) async-start(), calls=%async_computation.3 | async-start | bytes 131072 | tf_op jit(solution)/shard_map/psum | solution.py:138
  539.3 4.9 collective-permute-start.2
  542.9 5.7 collective-permute-start.3
  720.0 136.3 %all-gather.8.cloned.1.call-start = ((), (), s32[]{:S(2)}) async-start(), calls=%async_computation.4 | async-start | bytes 2162688 | tf_op jit(solution)/shard_map/all_gather | solution.py:25
  778.6 218.5 %all-reduce.17.cloned.1.call-start = ((), (), s32[]{:S(2)}) async-start(), calls=%async_computation.5 | async-start | bytes 131072 | tf_op jit(solution)/shard_map/psum | solution.py:103
  939.1 298.2 %all-reduce.19.cloned.1.call-start = ((), (), s32[]{:S(2)}) async-start(), calls=%async_computation.6 | async-start | bytes 131072 | tf_op jit(solution)/shard_map/psum | solution.py:138
  997.1 10.2 copy-start.4
  998.0 4.9 collective-permute-start.4
  1001.6 5.7 collective-permute-start.5
  1178.8 136.2 %all-gather.10.cloned.1.call-start = ((), (), s32[]{:S(2)}) async-start(), calls=%async_computation.7 | async-start | bytes 2162688 | tf_op jit(solution)/shard_map/all_gather | solution.py:25
  1237.3 218.3 %all-reduce.21.cloned.1.call-start = ((), (), s32[]{:S(2)}) async-start(), calls=%async_computation.8 | async-start | bytes 131072 | tf_op jit(solution)/shard_map/psum | solution.py:103
  1455.7 10.3 copy-start.6
  1456.6 175.3 %copy-start.5 = (f32[128,256]{1,0:T(8,128)S(1)}, f32[128,256]{1,0:T(8,128)}, u32[]{:S(2)}) copy-start(f32[128,256]{1,0:T(8,128)} %get-tuple-element.725) | copy-start | bytes 393220
  1456.6 5.0 collective-permute-start.6
  1460.3 5.7 collective-permute-start.7
Sparse Core Ops, SparseCore 0:
  9.7 65.5 all-reduce.10
  185.1 57.6 all-reduce.22
  245.4 75.2 all-gather.11
  323.1 75.1 all-gather.5
  480.5 57.8 all-reduce.12
  720.2 58.4 all-reduce.14
  781.2 75.1 all-gather.7
  939.3 57.8 all-reduce.16
  1178.9 58.4 all-reduce.18
  1239.8 75.1 all-gather.9
  1397.8 57.8 all-reduce.20
where the time goes:
time: 1650 us; the launch traced here: 1640 us
  waiting for transfers between devices  702 us (43%)
  blocking collectives  674 us (41%)
  matrix products  116 us (7%)
  local copies, waits for them, and re-layouts  91.5 us (6%)
  other arithmetic  20.7 us (1%)
  starting transfers between devices  18.2 us (1%)
    all_gather x4, waiting for transfers between devices, entering(): pieces = jax.tree.map(lambda part: lax.all_gather(part, axis), value)  302 us
    psum x4, blocking collectives, lengths(): lax.psum(jnp.sum(vector * vector, axis=1), ('sec', 'blk')) + epsilon  300 us
    psum x3, blocking collectives, local(): lax.psum(jnp.sum(product[None] * stacked, axis=2), ('sec', 'blk'))  250 us
    psum x4, waiting for transfers between devices, operator(): lax.psum(jnp.dot(rounded, ahead_panel, preferred_element_type=jnp.float32...  207 us
    psum x2, waiting for transfers between devices, local(): lax.psum(jnp.dot(precondition_folded, selector, precision=highest), 'blk')  117 us
    dot_general x93, matrix products, compose(): jnp.dot(first_value, second_map.T, precision=highest) + second_value  97.7 us
    dynamic_slice x186, local copies, waits for them, and re-layouts, step(): longer = join(so_far, jax.tree.map(lambda part: part[position], pieces))  87 us
    all_gather x4, blocking collectives, operator(): lax.all_gather(rounded, 'blk', axis=1, tiled=True)  69.6 us
  transfers between devices with their start and end apart: 19, of which 15 were waited for; matrix products, arithmetic and copies ran while one was open for 1% of the time, Pallas kernels for 0%

commit v1 on v0

--- a/solution.py
+++ b/solution.py
@@ -5,6 +5,23 @@
 
 KRYLOV = 3
 epsilon = 1e-06
+
+
+def get_columns_up(chunk, device_axis):
+    n_lanes = lax.psum(1, device_axis)
+    xs_all = [(at, (at + 1) % n_lanes) for at in range(n_lanes)]
+    block_list = [(at, (at - 1) % n_lanes) for at in range(n_lanes)]
+    front, spare = ([chunk], [chunk])
+    for _ in range(n_lanes // 2):
+        kept_arr = lax.ppermute(front[-1], device_axis, xs_all)
+        front.append(kept_arr)
+    rr = 0
+    while rr < (n_lanes - 1) // 2:
+        main = lax.ppermute(spare[-1], device_axis, block_list)
+        spare.append(main)
+        rr += 1
+    out_arr = jnp.concatenate([*front[::-1], *spare[1:]], axis=1)
+    return jnp.roll(out_arr, (lax.axis_index(device_axis) - n_lanes // 2) * chunk.shape[1], axis=1)
 
 
 def extended(x, sides, width):
@@ -130,7 +147,7 @@
     for column in range(KRYLOV):
         precondition_rounded = basis[column].astype(jnp.bfloat16)
         precondition_folded = lax.dot_general(
-            lax.all_gather(precondition_rounded, "blk", axis=1, tiled=True),
+            get_columns_up(precondition_rounded, "blk"),
             block_inverse,
             contract,
             preferred_element_type=jnp.float32,

time: 1650 us -> 1680 us (1.018)
  waiting for transfers between devices: 702 us -> 743 us
  blocking collectives: 674 us -> 635 us
  starting transfers between devices: 18.2 us -> 48.9 us
    all_gather x3 -> x0, blocking collectives: 41.1 us -> none  [local(): lax.all_gather(precondition_rounded, 'blk', axis=1, tiled=True)]
    ppermute x0 -> x21, starting transfers between devices: none -> 30.7 us  [the longest x12 18.6 us: get_columns_up(): kept_arr = lax.ppermute(front[-1], device_axis, xs_all)]
  transfers between devices with their start and end apart: 19 -> 40, of which waited for: 15 -> 29; matrix products, arithmetic and copies ran while one was open for 1% -> 1% of each run, Pallas kernels for 0% -> 0%
where the time goes in v1:
time: 1680 us; the launch traced here: 1670 us
  waiting for transfers between devices  743 us (44%)
  blocking collectives  635 us (38%)
  matrix products  117 us (7%)
  local copies, waits for them, and re-layouts  91.9 us (5%)
  starting transfers between devices  48.9 us (3%)
  other arithmetic  20.3 us (1%)
    all_gather x4, waiting for transfers between devices, entering(): pieces = jax.tree.map(lambda part: lax.all_gather(part, axis), value)  302 us
    psum x4, blocking collectives, lengths(): lax.psum(jnp.sum(vector * vector, axis=1), ('sec', 'blk')) + epsilon  300 us
    psum x3, blocking collectives, local(): lax.psum(jnp.sum(product[None] * stacked, axis=2), ('sec', 'blk'))  250 us
    psum x4, waiting for transfers between devices, operator(): lax.psum(jnp.dot(rounded, ahead_panel, preferred_element_type=jnp.float32...  220 us
    psum x2, waiting for transfers between devices, local(): lax.psum(jnp.dot(precondition_folded, selector, precision=highest), 'blk')  128 us
    dot_general x93, matrix products, compose(): jnp.dot(first_value, second_map.T, precision=highest) + second_value  97.7 us
    dynamic_slice x186, local copies, waits for them, and re-layouts, step(): longer = join(so_far, jax.tree.map(lambda part: part[position], pieces))  87 us
    all_gather x4, blocking collectives, operator(): lax.all_gather(rounded, 'blk', axis=1, tiled=True)  69.6 us
  transfers between devices with their start and end apart: 40, of which 29 were waited for; matrix products, arithmetic and copies ran while one was open for 1% of the time, Pallas kernels for 0%

profile of v1, /device:TPU:1, one launch (start us, length us, event | category | flops | bytes accessed | tf_op | source)
XLA Modules:
  0.0 1674.0 jit_solution(3170806978275346151)
XLA Ops:
  9.4 16.2 all_gather.43
  27.7 47.5 %all-reduce.11.cloned.1.call-done = f32[1,128,128]{1,2,0:T(8,128)} async-done(((f32[1,128,128]{1,2,0:T(8,128)}), f32[1,128,128]{1,2,0:T(8,128)}) %all-reduce.11.cloned.1.call-update) | async-done | bytes 65552 | tf_op jit(solution)/shard_map/psum | solution.py:120
  80.7 4.2 collective-permute-done.1
  85.3 83.2 %psum.106 = f32[128]{0:T(128)S(1)} all-reduce(f32[128]{0:T(128)S(1)} %get-tuple-element.721), channel_id=1, replica_groups=mesh['sec'=32,'blk'=8] {'sec','blk'}, use_global_device_ids=true, to_apply=%region_4.5 | all-reduce | flops 128 | bytes 1024 | tf_op jit(solution)/shard_map/psum | solution.py:138
  172.3 15.1 all_gather.44
  195.3 3.5 collective-permute-done.8
  200.4 59.6 %all-reduce.23.cloned.1.call-done = (f32[128,128]{1,0:T(8,128)}, f32[1,128,128]{2,1,0:T(8,128)}) async-done(((f32[128,128]{1,0:T(8,128)}, f32[1,128,128]{2,1,0:T(8,128)}), (f32[128,128]{1,0:T(8,128)}, f32[1,128,128]{2,1,0:T(8,128)})) %all-reduce.23.cloned.1.call-update) | async-done | bytes 131088 | tf_op jit(solution)/shard_map/psum | solution.py:99
  262.2 75.7 %all-gather.12.cloned.1.call-done = f32[4096,128]{1,0:T(8,128)} async-done(((f32[128,128]{1,0:T(8,128)}), f32[4096,128]{1,0:T(8,128)}) %all-gather.12.cloned.1.call-update) | async-done | bytes 2097168 | tf_op jit(solution)/shard_map/all_gather | solution.py:42
  337.9 77.6 %all-gather.6.cloned.1.call-done = f32[32,128,128]{2,1,0:T(8,128)} async-done(((f32[1,128,128]{2,1,0:T(8,128)}), f32[32,128,128]{2,1,0:T(8,128)}) %all-gather.6.cloned.1.call-update) | async-done | bytes 2097168 | tf_op jit(solution)/shard_map/all_gather | solution.py:42
  415.5 63.2 %while.64 = (s32[]{:T(128)}, f32[128,128]{0,1:T(8,128)S(1)}, s32[]{:T(128)}, f32[32,128,128]{2,1,0:T(8,128)}, f32[32,128,128]{2,1,0:T(8,128)}, /*index=5*/s32[]{:T(128)}, s32[]{:T(128)}) while((s32[]{:T(128)}, f32[128,128]{0,1:T(8,128)S(1)}, s32[]{:T(128)}, f32[32,128,128]{2,1,0:T(8,128)}, f32[32,128,128]{2,1,0:T(8,128)}, ...), condition=%wide.region_8.10_spmd.clone, body=%wide.region_7.9_spmd.clone.sunk | while | flops 25231364 | bytes 723043 | solution.py:51
  479.1 17.8 %all_gather.49 = bf16[128,2048]{1,0:T(8,128)(2,1)S(1)} all-gather(bf16[128,256]{1,0:T(8,128)(2,1)S(1)} %get-tuple-element.723), channel_id=1, replica_groups=mesh['sec'=32,'blk'=8] {'blk'}, dimensions={1}, use_global_device_ids=true | all-gather | bytes 589824 | tf_op jit(solution)/shard_map/all_gather | solution.py:118
  498.1 57.6 %all-reduce.13.cloned.1.call-done = f32[1,128,128]{2,1,0:T(8,128)} async-done(((f32[1,128,128]{2,1,0:T(8,128)}), f32[1,128,128]{2,1,0:T(8,128)}) %all-reduce.13.cloned.1.call-update) | async-done | bytes 65552 | tf_op jit(solution)/shard_map/psum | solution.py:120
  561.6 4.2 collective-permute-done.10
  566.4 83.2 %psum.110 = f32[1,128]{1,0:T(1,128)S(1)} all-reduce(f32[1,128]{1,0:T(1,128)S(1)} %bitcast.284), channel_id=1, replica_groups=mesh['sec'=32,'blk'=8] {'sec','blk'}, use_global_device_ids=true, to_apply=%region_11.13 | all-reduce | flops 128 | bytes 1024 | tf_op jit(solution)/shard_map/psum | solution.py:166
  649.8 72.3 %psum.111 = f32[128]{0:T(128)S(1)} all-reduce(f32[128]{0:T(128)S(1)} %get-tuple-element.688), channel_id=1, replica_groups=mesh['sec'=32,'blk'=8] {'sec','blk'}, use_global_device_ids=true, to_apply=%region_13.15 | all-reduce | flops 128 | bytes 1024 | tf_op jit(solution)/shard_map/psum | solution.py:138
  740.1 63.9 %all-reduce.15.cloned.1.call-done = f32[1,128,128]{2,1,0:T(8,128)} async-done(((f32[1,128,128]{2,1,0:T(8,128)}), f32[1,128,128]{2,1,0:T(8,128)}) %all-reduce.15.cloned.1.call-update) | async-done | bytes 65552 | tf_op jit(solution)/shard_map/psum | solution.py:155
  804.1 77.7 %all-gather.8.cloned.1.call-done = f32[32,128,128]{2,1,0:T(8,128)} async-done(((f32[1,128,128]{2,1,0:T(8,128)}), f32[32,128,128]{2,1,0:T(8,128)}) %all-gather.8.cloned.1.call-update) | async-done | bytes 2097168 | tf_op jit(solution)/shard_map/all_gather | solution.py:42
  881.7 63.2 %while.65 = (s32[]{:T(128)}, f32[128,128]{0,1:T(8,128)S(1)}, s32[]{:T(128)}, f32[32,128,128]{2,1,0:T(8,128)}, f32[32,128,128]{2,1,0:T(8,128)}, /*index=5*/s32[]{:T(128)}, s32[]{:T(128)}) while((s32[]{:T(128)}, f32[128,128]{0,1:T(8,128)S(1)}, s32[]{:T(128)}, f32[32,128,128]{2,1,0:T(8,128)}, f32[32,128,128]{2,1,0:T(8,128)}, ...), condition=%wide.region_16.18_spmd.clone, body=%wide.region_15.17_spmd.clone.sunk | while | flops 25231364 | bytes 723043 | solution.py:51
  945.9 17.8 %all_gather.52 = bf16[128,2048]{1,0:T(8,128)(2,1)S(1)} all-gather(bf16[128,256]{1,0:T(8,128)(2,1)S(1)} %get-tuple-element.725), channel_id=1, replica_groups=mesh['sec'=32,'blk'=8] {'blk'}, dimensions={1}, use_global_device_ids=true | all-gather | bytes 589824 | tf_op jit(solution)/shard_map/all_gather | solution.py:118
  964.9 57.6 %all-reduce.17.cloned.1.call-done = f32[1,128,128]{2,1,0:T(8,128)} async-done(((f32[1,128,128]{2,1,0:T(8,128)}), f32[1,128,128]{2,1,0:T(8,128)}) %all-reduce.17.cloned.1.call-update) | async-done | bytes 65552 | tf_op jit(solution)/shard_map/psum | solution.py:120
  1023.4 3.2 collective-permute-start.18
  1028.6 4.2 collective-permute-done.19
  1033.3 83.2 %psum.114 = f32[2,128]{1,0:T(2,128)S(1)} all-reduce(f32[2,128]{1,0:T(2,128)S(1)} %multiply_reduce_fusion.3), channel_id=1, replica_groups=mesh['sec'=32,'blk'=8] {'sec','blk'}, use_global_device_ids=true, to_apply=%region_19.21 | all-reduce | flops 256 | bytes 2048 | tf_op jit(solution)/shard_map/psum | solution.py:166
  1116.8 72.3 %psum.115 = f32[128]{0:T(128)S(1)} all-reduce(f32[128]{0:T(128)S(1)} %get-tuple-element.684), channel_id=1, replica_groups=mesh['sec'=32,'blk'=8] {'sec','blk'}, use_global_device_ids=true, to_apply=%region_22.24 | all-reduce | flops 128 | bytes 1024 | tf_op jit(solution)/shard_map/psum | solution.py:138
  1207.1 63.9 %all-reduce.19.cloned.1.call-done = f32[1,128,128]{2,1,0:T(8,128)} async-done(((f32[1,128,128]{2,1,0:T(8,128)}), f32[1,128,128]{2,1,0:T(8,128)}) %all-reduce.19.cloned.1.call-update) | async-done | bytes 65552 | tf_op jit(solution)/shard_map/psum | solution.py:155
  1277.3 71.3 %all-gather.10.cloned.1.call-done = f32[32,128,128]{2,1,0:T(8,128)} async-done(((f32[1,128,128]{2,1,0:T(8,128)}), f32[32,128,128]{2,1,0:T(8,128)}) %all-gather.10.cloned.1.call-update) | async-done | bytes 2097168 | tf_op jit(solution)/shard_map/all_gather | solution.py:42
  1348.6 63.2 %while.66 = (s32[]{:T(128)}, f32[128,128]{0,1:T(8,128)S(1)}, s32[]{:T(128)}, f32[32,128,128]{2,1,0:T(8,128)}, f32[32,128,128]{2,1,0:T(8,128)}, /*index=5*/s32[]{:T(128)}, s32[]{:T(128)}) while((s32[]{:T(128)}, f32[128,128]{0,1:T(8,128)S(1)}, s32[]{:T(128)}, f32[32,128,128]{2,1,0:T(8,128)}, f32[32,128,128]{2,1,0:T(8,128)}, ...), condition=%wide.region_26.28_spmd.clone, body=%wide.region_25.27_spmd.clone.sunk | while | flops 25231364 | bytes 723043 | solution.py:51
  1412.8 17.8 %all_gather.55 = bf16[128,2048]{1,0:T(8,128)(2,1)S(1)} all-gather(bf16[128,256]{1,0:T(8,128)(2,1)S(1)} %get-tuple-element.727), channel_id=1, replica_groups=mesh['sec'=32,'blk'=8] {'blk'}, dimensions={1}, use_global_device_ids=true | all-gather | bytes 589824 | tf_op jit(solution)/shard_map/all_gather | solution.py:118
  1431.8 57.6 %all-reduce.21.cloned.1.call-done = f32[1,128,128]{2,1,0:T(8,128)} async-done(((f32[1,128,128]{2,1,0:T(8,128)}), f32[1,128,128]{2,1,0:T(8,128)}) %all-reduce.21.cloned.1.call-update) | async-done | bytes 65552 | tf_op jit(solution)/shard_map/psum | solution.py:120
  1495.5 4.2 collective-permute-done.28
  1500.9 83.2 %psum.118 = f32[3,128]{1,0:T(4,128)S(1)} all-reduce(f32[3,128]{1,0:T(4,128)S(1)} %multiply_reduce_fusion.1), channel_id=1, replica_groups=mesh['sec'=32,'blk'=8] {'sec','blk'}, use_global_device_ids=true, to_apply=%region_29.31 | all-reduce | flops 384 | bytes 3072 | tf_op jit(solution)/shard_map/psum | solution.py:166
  1584.3 72.3 %psum.119 = f32[128]{0:T(128)S(1)} all-reduce(f32[128]{0:T(128)S(1)} %multiply_reduce_fusion.4), channel_id=1, replica_groups=mesh['sec'=32,'blk'=8] {'sec','blk'}, use_global_device_ids=true, to_apply=%region_32.34 | all-reduce | flops 128 | bytes 1024 | tf_op jit(solution)/shard_map/psum | solution.py:138
  (583 shorter events, 287.4 us)
Async XLA Ops:
  6.5 68.6 %all-reduce.11.cloned.1.call-start = ((), (), s32[]{:S(2)}) async-start(), calls=%async_computation | async-start | bytes 131072 | tf_op jit(solution)/shard_map/psum | solution.py:120
  9.3 250.7 %all-reduce.23.cloned.1.call-start = ((), (), s32[]{:S(2)}) async-start(), calls=%async_computation.10 | async-start | bytes 262144 | tf_op jit(solution)/shard_map/psum | solution.py:99
  76.1 4.4 collective-permute-start
  79.1 5.7 collective-permute-start.1
  170.3 17.4 %collective-permute-start.3 = (bf16[128,256]{1,0:T(8,128)(2,1)S(1)}, bf16[128,256]{1,0:T(8,128)(2,1)S(1)}, u32[]{:S(2)}, u32[]{:S(2)}) collective-permute-start(bf16[128,256]{1,0:T(8,128)(2,1)S(1)} %collective-permute-done.2), channel_id=1, source_target_pairs={{0,1},{1,2},{2,3},{3,4},{4,5},{5,6},{6,7},{7,0},{8,9},{9,10},{10,1... | collective-permute-start | bytes 196616 | tf_op jit(solution)/shard_map/ppermute | solution.py:16
  187.5 4.0 collective-permute-start.6
  187.6 3.8 collective-permute-start.4
  200.4 137.5 %all-gather.12.cloned.1.call-start = ((), (), s32[]{:S(2)}) async-start(), calls=%async_computation.9 | async-start | bytes 2162688 | tf_op jit(solution)/shard_map/all_gather | solution.py:42
  261.5 154.0 %all-gather.6.cloned.1.call-start = ((), (), s32[]{:S(2)}) async-start(), calls=%async_computation.1 | async-start | bytes 2162688 | tf_op jit(solution)/shard_map/all_gather | solution.py:42
  262.1 293.6 %all-reduce.13.cloned.1.call-start = ((), (), s32[]{:S(2)}) async-start(), calls=%async_computation.2 | async-start | bytes 131072 | tf_op jit(solution)/shard_map/psum | solution.py:120
  497.7 306.3 %all-reduce.15.cloned.1.call-start = ((), (), s32[]{:S(2)}) async-start(), calls=%async_computation.3 | async-start | bytes 131072 | tf_op jit(solution)/shard_map/psum | solution.py:155
  556.6 4.9 collective-permute-start.9
  560.1 5.7 collective-permute-start.10
  724.7 3.9 collective-permute-start.12
  727.0 3.7 collective-permute-start.15
  728.5 4.9 collective-permute-start.13
  733.4 4.9 collective-permute-start.14
  734.4 4.1 collective-permute-start.17
  740.0 141.7 %all-gather.8.cloned.1.call-start = ((), (), s32[]{:S(2)}) async-start(), calls=%async_computation.4 | async-start | bytes 2162688 | tf_op jit(solution)/shard_map/all_gather | solution.py:42
  804.0 218.5 %all-reduce.17.cloned.1.call-start = ((), (), s32[]{:S(2)}) async-start(), calls=%async_computation.5 | async-start | bytes 131072 | tf_op jit(solution)/shard_map/psum | solution.py:120
  964.5 306.5 %all-reduce.19.cloned.1.call-start = ((), (), s32[]{:S(2)}) async-start(), calls=%async_computation.6 | async-start | bytes 131072 | tf_op jit(solution)/shard_map/psum | solution.py:155
  1023.4 5.1 collective-permute-start.18
  1027.2 5.7 collective-permute-start.19
  1191.6 3.9 collective-permute-start.21
  1194.0 3.7 collective-permute-start.24
  1195.5 4.9 collective-permute-start.22
  1200.4 4.9 collective-permute-start.23
  1201.4 4.1 collective-permute-start.26
  1207.0 141.6 %all-gather.10.cloned.1.call-start = ((), (), s32[]{:S(2)}) async-start(), calls=%async_computation.7 | async-start | bytes 2162688 | tf_op jit(solution)/shard_map/all_gather | solution.py:42
  1271.0 218.3 %all-reduce.21.cloned.1.call-start = ((), (), s32[]{:S(2)}) async-start(), calls=%async_computation.8 | async-start | bytes 131072 | tf_op jit(solution)/shard_map/psum | solution.py:120
  1490.3 5.0 collective-permute-start.27
  1494.0 5.7 collective-permute-start.28
  (20 other events, 923.7 us)
Sparse Core Ops, SparseCore 0:
  9.7 65.4 all-reduce.10
  200.5 59.4 all-reduce.22
  262.6 75.2 all-gather.11
  340.3 75.1 all-gather.5
  497.8 57.8 all-reduce.12
  740.2 63.7 all-reduce.14
  806.6 75.1 all-gather.7
  964.6 57.8 all-reduce.16
  1207.2 63.8 all-reduce.18
  1273.5 75.1 all-gather.9
  1431.5 57.8 all-reduce.20
